TPU v7x, 32 devices: a whole 2x2x4 slice. The times are simulated.
32 devices in a mesh: blk: 8 (over z, y), plane: 4 (over x, core).
Axes of the slice: x: 2, y: 2, z: 4, core: 2. Of those that a mesh axis runs over, the one named last changes fastest.
Arguments:
- tiles: bfloat16 [128, 24, 128, 128], P(('blk', 'plane')), may hold values from -0.25 to 0.25
- tile_cols: int32 [128, 24], P(('blk', 'plane')), may hold values from 0 to 511
- tile_count: int32 [128], P(('blk', 'plane')), may hold values from 18 to 24, as said below
- u_start: float32 [16384], P(('blk', 'plane')), may hold values from -0.046875 to 0.046875
- v_start: float32 [65536], P(('blk', 'plane')), may hold values from -0.0234375 to 0.0234375
- beta_start: float32 [1], replicated, may hold values from 0.5 to 1.5
- left_basis: float32 [16384, 128], P(('blk', 'plane')), may hold values from -0.046875 to 0.046875
- right_basis: float32 [65536, 128], P(('blk', 'plane')), may hold values from -0.0234375 to 0.0234375
Outputs:
- left_vectors: float32 [1, 16384], P(None, ('blk', 'plane'))
- right_vectors: float32 [1, 65536], P(None, ('blk', 'plane'))
- coefficients: float32 [2], replicated
Inputs may be any that keep to these rules, and one draw needn't show every extreme that they name: `tile_count`: slots at and after a row block's count are padding; some row block uses all 24 slots.
All inputs are finite; a program needn't handle non-finite values.
Results may differ from a plain program's by a relative error of at most 0.00055.
The roundings to bfloat16 on the way count: a program that leaves them out, or rounds other values in their place, can miss the bound.
Values may be sent and summed in bfloat16 or wider, within the bound.
No kernel may reach another device: no remote copies, remote signals or barrier semaphores. Data moves between devices by JAX's collectives and lax.ppermute only.
A program may use at most 64 MiB of HBM per device.

v0:
```python
import math

import jax
import jax.numpy as jnp
from jax import lax
from jax.sharding import PartitionSpec as P


def project_twice(vec, basis, gram):
    high = lax.Precision.HIGHEST
    first, whole_sq = lax.psum(
        (jnp.dot(vec, basis, precision=high), jnp.sum(vec * vec)), ("blk", "plane")
    )
    coef = 2.0 * first - jnp.dot(gram, first, precision=high)
    vec = vec - jnp.dot(basis, coef, precision=high)
    total = (
        whole_sq - 2.0 * jnp.sum(coef * first) + jnp.sum(coef * jnp.dot(gram, coef, precision=high))
    )
    norm = jnp.sqrt(total + 1e-06)
    return (vec / norm, norm)


def on_device(tiles, tile_cols, tile_count, u_start, v_start, beta_start, left_basis, right_basis):
    high = lax.Precision.HIGHEST
    devices = lax.axis_size(("blk", "plane"))
    blocks, slots = tile_cols.shape
    n_tiles = v_start.shape[0] * devices // 128
    live = (lax.iota(jnp.int32, slots)[None, :] < tile_count[:, None]).astype(jnp.float32)
    onehot = (tile_cols.reshape(-1)[:, None] == lax.iota(jnp.int32, n_tiles)[None, :]).astype(
        jnp.float32
    )
    left_gram, right_gram = lax.psum(
        (
            jnp.dot(left_basis.T, left_basis, precision=high),
            jnp.dot(right_basis.T, right_basis, precision=high),
        ),
        ("blk", "plane"),
    )
    left_scale = math.sqrt(u_start.shape[0] * devices)
    right_scale = math.sqrt(v_start.shape[0] * devices)
    vec_right = v_start
    vec_left = u_start
    beta = beta_start[0]
    lefts, rights, coefs = ([], [], [])
    rounded = vec_right.astype(jnp.bfloat16)
    whole = lax.all_gather(rounded, ("blk", "plane"), axis=0, tiled=True)
    table = whole.reshape(n_tiles, 128)
    picked = jnp.take(table, tile_cols, axis=0)
    values = jnp.einsum("rsij,rsj->rsi", tiles, picked, preferred_element_type=jnp.float32)
    forward_out = jnp.sum(values * live[:, :, None], axis=1).reshape(-1)
    vec_left, alpha = project_twice(forward_out - beta * vec_left, left_basis, left_gram)
    left_rows = vec_left.astype(jnp.bfloat16).reshape(blocks, 128)
    contrib = jnp.einsum("rsij,ri->rsj", tiles, left_rows, preferred_element_type=jnp.float32)
    contrib = (contrib * live[:, :, None]).reshape(-1, 128)
    partial_value = lax.dot_general(onehot, contrib, (((0,), (0,)), ((), ())), precision=high)
    owned = lax.psum_scatter(partial_value, ("blk", "plane"), scatter_dimension=0, tiled=True)
    back_out = owned.reshape(-1)
    vec_right, beta = project_twice(back_out - alpha * vec_right, right_basis, right_gram)
    lefts.append(vec_left * left_scale)
    rights.append(vec_right * right_scale)
    coefs.append(alpha)
    coefs.append(beta)
    return (jnp.stack(lefts), jnp.stack(rights), jnp.stack(coefs))


def solution(mesh):
    placed = (
        P(("blk", "plane"), None, None, None),
        P(("blk", "plane"), None),
        P(("blk", "plane")),
        P(("blk", "plane")),
        P(("blk", "plane")),
        P(),
        P(("blk", "plane"), None),
        P(("blk", "plane"), None),
    )
    return jax.shard_map(
        on_device,
        mesh=mesh,
        in_specs=placed,
        out_specs=(P(None, ("blk", "plane")), P(None, ("blk", "plane")), P()),
        check_vma=False,
    )
```

profile of v0, /device:TPU:0, one launch (start us, length us, event | category | flops | bytes accessed | tf_op | source)
XLA Modules:
  0.0 338.0 jit_solution(10103056694969738724)
XLA Ops:
  7.2 0.0 copy-start
  7.2 0.0 all-reduce.5.cloned.1.call-start
  7.2 2.4 fusion.21
  9.6 0.0 copy-start.1
  9.6 4.1 %fusion.22 = f32[128,128]{1,0:T(8,128)} fusion(f32[2048,128]{1,0:T(8,128)} %param.15), kind=kOutput, calls=%fused_computation.48 | convolution fusion | flops 402653184 | bytes 1114112 | tf_op jit(solution)/shard_map/dot_general | solution.py:35
  13.7 0.0 all-reduce.5.cloned.1.call-update
  13.7 0.0 reduce-scatter.2.cloned.1.call-start
  13.8 0.7 compare_and_fusion
  14.5 0.8 eq.15
  15.2 0.7 compare_select_fusion
  16.6 0.7 fusion.12
  17.3 0.1 reshape.56
  17.4 0.7 convert_element_type.14
  18.1 43.6 %all_gather.3 = bf16[65536]{0:T(1024)(128)(2,1)S(1)} all-gather(bf16[2048]{0:T(1024)(128)(2,1)S(1)} %convert_element_type.14), channel_id=1, replica_groups=mesh['blk'=8,'plane'=4] {'blk','plane'}, dimensions={0}, use_global_device_ids=true | all-gather | bytes 135168 | tf_op jit(solution)/shard_map/all_gather | solution.py:46
  61.7 1.3 gather_fusion
  62.9 0.8 select_bitcast_fusion
  63.8 0.0 copy-done
  63.8 0.0 copy-start.3
  63.8 1.7 fusion.8
  65.5 0.1 multiply_reduce_fusion
  65.6 1.3 multiply_reduce_fusion.2
  66.9 0.0 copy-done.1
  66.9 0.2 convolution_bitcast_fusion.1
  67.1 37.2 %all-reduce.1 = (f32[128]{0:T(128)S(1)}, f32[]{:T(128)}) all-reduce(f32[128]{0:T(128)S(1)} %convolution_bitcast_fusion.1, f32[]{:T(128)} %get-tuple-element.13), channel_id=1, replica_groups=mesh['blk'=8,'plane'=4] {'blk','plane'}, use_global_device_ids=true, to_apply=%region_1.0 | all-reduce | flops 129 | bytes 1032 | tf_op jit(solution)/shard_map/psum | solution.py:11
  104.3 37.2 %all-reduce.5.cloned.1.call-done = (f32[128,128]{1,0:T(8,128)}, f32[128,128]{1,0:T(8,128)}) async-done(((f32[128,128]{1,0:T(8,128)}, f32[128,128]{1,0:T(8,128)}), (f32[128,128]{1,0:T(8,128)}, f32[128,128]{1,0:T(8,128)})) %all-reduce.5.cloned.1.call-update) | async-done | bytes 131088 | tf_op jit(solution)/shard_map/psum | solution.py:32
  141.5 0.0 copy-start.2
  141.5 1.7 multiply_reduce_fusion.4
  143.2 1.7 fusion.4
  144.9 0.3 fusion.18
  147.2 0.5 fusion.10
  147.7 0.1 broadcast_multiply_fusion
  147.8 1.2 fusion.6
  148.9 0.0 reduce-scatter.2.cloned.1.call-update
  149.0 0.6 broadcast_multiply_fusion.1
  149.6 134.2 %reduce-scatter.2.cloned.1.call-done = f32[16,128]{1,0:T(8,128)} async-done(((f32[512,128]{1,0:T(8,128)}), f32[16,128]{1,0:T(8,128)}) %reduce-scatter.2.cloned.1.call-update) | async-done | bytes 8208 | tf_op jit(solution)/shard_map/reduce_scatter | solution.py:56
  283.8 0.0 copy-done.3
  283.8 1.3 multiply_reduce_fusion.1
  285.1 1.8 convolution_bitcast_fusion
  286.9 37.1 %all-reduce = (f32[128]{0:T(128)S(1)}, f32[]{:T(128)}) all-reduce(f32[128]{0:T(128)S(1)} %convolution_bitcast_fusion, f32[]{:T(128)} %get-tuple-element.9), channel_id=1, replica_groups=mesh['blk'=8,'plane'=4] {'blk','plane'}, use_global_device_ids=true, to_apply=%region_8.9 | all-reduce | flops 129 | bytes 1032 | tf_op jit(solution)/shard_map/psum | solution.py:11
  324.0 0.0 copy-done.2
  324.0 0.8 multiply_reduce_fusion.3
  324.9 0.9 fusion.5
  325.8 2.2 fusion.14
  330.0 0.6 divide_multiply_fusion
  330.6 0.6 pad_maximum_fusion
  (2 shorter events, 0.0 us)
Async XLA Ops:
  7.2 56.6 %copy-start = (bf16[4,24,128,128]{3,2,1,0:T(8,128)(2,1)S(1)}, bf16[4,24,128,128]{3,2,1,0:T(8,128)(2,1)}, u32[]{:S(2)}) copy-start(bf16[4,24,128,128]{3,2,1,0:T(8,128)(2,1)} %param.8) | copy-start | bytes 9437188
  7.2 134.3 %all-reduce.5.cloned.1.call-start = ((), (), s32[]{:S(2)}) async-start(), calls=%async_computation.2 | async-start | bytes 262144 | tf_op jit(solution)/shard_map/psum | solution.py:32
  9.6 57.3 %copy-start.1 = (f32[512,128]{1,0:T(8,128)S(1)}, f32[512,128]{1,0:T(8,128)}, u32[]{:S(2)}) copy-start(f32[512,128]{1,0:T(8,128)} %param.14) | copy-start | bytes 786436
  13.7 270.1 %reduce-scatter.2.cloned.1.call-start = ((), (), s32[]{:S(2)}) async-start(), calls=%async_computation.1 | async-start | bytes 270336 | tf_op jit(solution)/shard_map/reduce_scatter | solution.py:56
  63.8 220.0 %copy-start.3 = (f32[2048]{0:T(1024)S(1)}, f32[2048]{0:T(1024)}, u32[]{:S(2)}) copy-start(f32[2048]{0:T(1024)} %param.12) | copy-start | bytes 24580
  141.5 182.5 %copy-start.2 = (f32[128,128]{1,0:T(8,128)S(1)}, f32[128,128]{1,0:T(8,128)}, u32[]{:S(2)}) copy-start(f32[128,128]{1,0:T(8,128)} %get-tuple-element.8) | copy-start | bytes 196612
Sparse Core Ops, SparseCore 0:
  13.9 127.5 all-reduce.4
  149.1 134.6 reduce-scatter.1
where the time goes:
time: 340 us; the launch traced here: 338 us
  waiting for transfers between devices  171 us (50%)
  blocking collectives  118 us (35%)
  matrix products  19.5 us (6%)
  between operations  18.8 us (6%)
  other arithmetic  8.19 us (2%)
    reduce_scatter x1, waiting for transfers between devices, on_device(): lax.psum_scatter(partial_value, ('blk', 'plane'), scatter_dimension=0, ti...  134 us
    psum x2, blocking collectives, project_twice(): lax.psum((jnp.dot(vec, basis, precision=high), jnp.sum(vec * vec)), ('blk...  74.3 us
    all_gather x1, blocking collectives, on_device(): whole = lax.all_gather(rounded, ('blk', 'plane'), axis=0, tiled=True)  43.6 us
    psum x1, waiting for transfers between devices, on_device(): lax.psum((jnp.dot(left_basis.T, left_basis, precision=high), jnp.dot(righ...  37.2 us
  transfers between devices with their start and end apart: 2, of which 2 were waited for; matrix products, arithmetic and copies ran while one was open for 3% of the time, Pallas kernels for 0%

commit v1 on v0

v1 whole, which is shorter than its diff:
```python
import math

import jax
import jax.numpy as jnp
from jax import lax
from jax.sharding import PartitionSpec as P

AXES = ("blk", "plane")


def exchange(parts):
    return lax.all_to_all(parts, AXES, 0, 0, tiled=True)


def spread(rows, devices):
    return jnp.broadcast_to(rows[None], (devices,) + rows.shape)


def finish(vec, basis, gram, first, whole_sq):
    high = lax.Precision.HIGHEST
    coef = 2.0 * first - jnp.dot(gram, first, precision=high)
    vec = vec - jnp.dot(basis, coef, precision=high)
    total = (
        whole_sq - 2.0 * jnp.sum(coef * first) + jnp.sum(coef * jnp.dot(gram, coef, precision=high))
    )
    norm = jnp.sqrt(total + 1e-06)
    return (vec / norm, norm)


def inner(vec, basis):
    first = jnp.dot(vec, basis, precision=lax.Precision.HIGHEST)
    square = jnp.broadcast_to(jnp.sum(vec * vec), first.shape)
    return jnp.stack([first, square])


def on_device(tiles, tile_cols, tile_count, u_start, v_start, beta_start, left_basis, right_basis):
    high = lax.Precision.HIGHEST
    devices = lax.axis_size(AXES)
    blocks, slots = tile_cols.shape
    width = tiles.shape[-1]
    kept = left_basis.shape[1]
    own_tiles = v_start.shape[0] // width
    n_tiles = own_tiles * devices
    live = (lax.iota(jnp.int32, slots)[None, :] < tile_count[:, None]).astype(jnp.float32)
    onehot = (tile_cols.reshape(-1)[:, None] == lax.iota(jnp.int32, n_tiles)[None, :]).astype(
        jnp.float32
    )
    left_scale = math.sqrt(u_start.shape[0] * devices)
    right_scale = math.sqrt(v_start.shape[0] * devices)
    beta = beta_start[0]

    grams = jnp.concatenate(
        [
            jnp.dot(left_basis.T, left_basis, precision=high),
            jnp.dot(right_basis.T, right_basis, precision=high),
        ]
    )
    share = 2 * kept // devices
    rounded = lax.reduce_precision(v_start, 8, 7).reshape(own_tiles, width)
    got = exchange(
        jnp.concatenate([grams.reshape(devices, share, kept), spread(rounded, devices)], axis=1)
    )
    gram_rows = jnp.sum(got[:, :share], axis=0)
    table = got[:, share:].reshape(n_tiles, width).astype(jnp.bfloat16)
    picked = jnp.take(table, tile_cols, axis=0)
    values = jnp.einsum("rsij,rsj->rsi", tiles, picked, preferred_element_type=jnp.float32)
    forward_out = jnp.sum(values * live[:, :, None], axis=1).reshape(-1)
    vec_left = forward_out - beta * u_start

    got = exchange(spread(jnp.concatenate([gram_rows, inner(vec_left, left_basis)]), devices))
    whole_grams = got[:, :share].reshape(2 * kept, kept)
    sums = jnp.sum(got[:, share:], axis=0)
    vec_left, alpha = finish(vec_left, left_basis, whole_grams[:kept], sums[0], sums[1, 0])

    left_rows = vec_left.astype(jnp.bfloat16).reshape(blocks, width)
    contrib = jnp.einsum("rsij,ri->rsj", tiles, left_rows, preferred_element_type=jnp.float32)
    contrib = (contrib * live[:, :, None]).reshape(-1, width)
    partial_value = lax.dot_general(onehot, contrib, (((0,), (0,)), ((), ())), precision=high)
    got = exchange(partial_value.reshape(devices, own_tiles, width))
    back_out = jnp.sum(got, axis=0).reshape(-1)
    vec_right = back_out - alpha * v_start

    got = exchange(spread(inner(vec_right, right_basis), devices))
    sums = jnp.sum(got, axis=0)
    vec_right, beta = finish(vec_right, right_basis, whole_grams[kept:], sums[0], sums[1, 0])
    return (
        (vec_left * left_scale)[None],
        (vec_right * right_scale)[None],
        jnp.stack([alpha, beta]),
    )


def solution(mesh):
    placed = (
        P(AXES, None, None, None),
        P(AXES, None),
        P(AXES),
        P(AXES),
        P(AXES),
        P(),
        P(AXES, None),
        P(AXES, None),
    )
    return jax.shard_map(
        on_device,
        mesh=mesh,
        in_specs=placed,
        out_specs=(P(None, AXES), P(None, AXES), P()),
        check_vma=False,
    )
```

time: 340 us -> 95.4 us (0.28)
  waiting for transfers between devices: 171 us -> 29.5 us
  blocking collectives: 118 us -> 12.7 us
  between operations: 18.8 us -> 5.49 us
  starting transfers between devices: 0.08 us -> 13.3 us
  local copies, waits for them, and re-layouts: 2.13 us -> 6.21 us
    reduce_scatter x1 -> x0, waiting for transfers between devices: 134 us -> none  [on_device(): lax.psum_scatter(partial_value, ('blk', 'plane'), scatter_dimension=0, ti...]
    psum x2 -> x0, blocking collectives: 74.3 us -> none  [project_twice(): lax.psum((jnp.dot(vec, basis, precision=high), jnp.sum(vec * vec)), ('blk...]
    all_gather x1 -> x0, blocking collectives: 43.6 us -> none  [on_device(): whole = lax.all_gather(rounded, ('blk', 'plane'), axis=0, tiled=True)]
    psum x1 -> x0, waiting for transfers between devices: 37.2 us -> none  [on_device(): lax.psum((jnp.dot(left_basis.T, left_basis, precision=high), jnp.dot(righ...]
    all_to_all x0 -> x3, waiting for transfers between devices: none -> 29.5 us  [exchange(): return lax.all_to_all(parts, AXES, 0, 0, tiled=True)]
    all_to_all x0 -> x3, starting transfers between devices: none -> 13.3 us  [exchange(): return lax.all_to_all(parts, AXES, 0, 0, tiled=True)]
    all_to_all x0 -> x1, blocking collectives: none -> 12.7 us  [exchange(): return lax.all_to_all(parts, AXES, 0, 0, tiled=True)]
  transfers between devices with their start and end apart: 2 -> 3, of which waited for: 2 -> 3; matrix products, arithmetic and copies ran while one was open for 3% -> 1% of each run, Pallas kernels for 0% -> 0%
where the time goes in v1:
time: 95.4 us; the launch traced here: 94.6 us
  waiting for transfers between devices  29.5 us (31%)
  matrix products  18.9 us (20%)
  starting transfers between devices  13.3 us (14%)
  blocking collectives  12.7 us (13%)
  other arithmetic  8.45 us (9%)
  local copies, waits for them, and re-layouts  6.21 us (7%)
  between operations  5.49 us (6%)
    all_to_all x3, waiting for transfers between devices, exchange(): return lax.all_to_all(parts, AXES, 0, 0, tiled=True)  29.5 us
    all_to_all x3, starting transfers between devices, exchange(): return lax.all_to_all(parts, AXES, 0, 0, tiled=True)  13.3 us
    all_to_all x1, blocking collectives, exchange(): return lax.all_to_all(parts, AXES, 0, 0, tiled=True)  12.7 us
    dot_general x1, matrix products, on_device(): jnp.dot(right_basis.T, right_basis, precision=high)  3.48 us
    dot_general x2, matrix products, finish(): jnp.dot(gram, coef, precision=high)  3.33 us
    dot_general x2, matrix products, finish(): coef = 2.0 * first - jnp.dot(gram, first, precision=high)  3.33 us
    dot_general x2, matrix products, finish(): vec = vec - jnp.dot(basis, coef, precision=high)  2.48 us
    dot_general x2, matrix products, inner(): first = jnp.dot(vec, basis, precision=lax.Precision.HIGHEST)  2.06 us
  transfers between devices with their start and end apart: 3, of which 3 were waited for; matrix products, arithmetic and copies ran while one was open for 1% of the time, Pallas kernels for 0%

profile of v1, /device:TPU:0, one launch (start us, length us, event | category | flops | bytes accessed | tf_op | source)
XLA Modules:
  0.0 94.6 jit_solution(15308984921807512805)
XLA Ops:
  0.6 0.0 copy-start
  0.6 0.0 copy-start.3
  0.7 0.0 copy-start.4
  0.7 0.9 reduce-precision_bitcast_fusion
  1.5 3.5 %fusion.28 = f32[128,128]{1,0:T(8,128)S(1)} fusion(f32[2048,128]{1,0:T(8,128)} %param.15), kind=kOutput, calls=%fused_computation.63 | convolution fusion | flops 402653184 | bytes 1114112 | tf_op jit(solution)/shard_map/dot_general | solution.py:55
  5.0 0.0 copy-start.1
  5.0 1.7 %fusion.27 = f32[128,128]{1,0:T(8,128)S(1)} fusion(f32[512,128]{1,0:T(8,128)} %param.14), kind=kOutput, calls=%fused_computation.62 | convolution fusion | flops 100663296 | bytes 327680 | tf_op jit(solution)/shard_map/dot_general | solution.py:54
  6.7 0.8 pad_maximum_fusion
  7.5 7.4 %all-to-all-start = ((f32[32,24,128]{2,1,0:T(8,128)}), f32[32,24,128]{2,1,0:T(8,128)}, u32[]{:S(2)}, u32[]{:S(2)}) async-start(f32[32,24,128]{2,1,0:T(8,128)} %pad_maximum_fusion), calls=%async_computation | async-start | bytes 786432 | tf_op jit(solution)/shard_map/all_to_all | solution.py:12
  15.6 0.1 reshape.83
  15.7 0.1 fusion.14
  15.8 12.4 %all-to-all-done = f32[32,24,128]{2,1,0:T(8,128)} async-done(((f32[32,24,128]{2,1,0:T(8,128)}), f32[32,24,128]{2,1,0:T(8,128)}, u32[]{:S(2)}, u32[]{:S(2)}) %all-to-all-start) | async-done | bytes 393248 | tf_op jit(solution)/shard_map/all_to_all | solution.py:12
  28.2 1.0 %slice.74 = bf16[32,16,128]{2,1,0:T(8,128)(2,1)S(1)} slice(f32[32,24,128]{2,1,0:T(8,128)} %all-to-all-done), slice={[0:32], [8:24], [0:128]} | slice | bytes 262144 | tf_op jit(solution)/shard_map/slice | solution.py:64
  29.2 1.3 %gather_fusion = bf16[96,128]{1,0:T(8,128)(2,1)} fusion(bf16[512,128]{1,0:T(8,128)(2,1)S(1)} %bitcast.121, s32[1024]{0:T(1024)S(1)} %pad_clamp_fusion), kind=kCustom, calls=%fused_computation | custom fusion | bytes 49536 | tf_op jit(solution)/shard_map/jit(_take)/gather | solution.py:65
  30.4 0.8 select_bitcast_fusion
  31.3 1.7 %fusion.10 = f32[4,24,1,128]{3,2,1,0:T(1,128)S(1)} fusion(bf16[4,24,128,128]{3,2,1,0:T(8,128)(2,1)S(1)} %copy-done, bf16[4,24,128,1]{2,1,0,3:T(8,128)(2,1)S(1)} %select_bitcast_fusion), kind=kOutput, calls=%fused_computation.21 | convolution fusion | flops 3145728 | bytes 3219456 | tf_op jit(solution)/shard_map/rsij,rsj->rsi/dot_general | solution.py:66
  33.0 0.1 multiply_reduce_fusion
  33.1 1.3 %multiply_reduce_fusion.2 = (f32[]{:T(128)}, f32[512]{0:T(512)S(1)}) fusion(f32[512]{0:T(512)} %param.11, f32[]{:T(128)} %bitcast.120, f32[4,128]{1,0:T(4,128)S(1)} %multiply_reduce_fusion), kind=kLoop, calls=%fused_computation.39 | loop fusion | flops 2047 | bytes 6152 | tf_op jit(solution)/shard_map/reduce_sum | solution.py:32
  34.4 0.2 fusion.29
  34.6 0.7 pad.5.clone
  35.4 0.9 slice_reduce_fusion
  36.3 0.1 maximum_maximum_fusion
  36.4 0.7 broadcast_in_dim.47
  37.1 3.3 %all-to-all-start.1 = ((f32[32,10,128]{2,1,0:T(8,128)}), f32[32,10,128]{2,1,0:T(8,128)}, u32[]{:S(2)}, u32[]{:S(2)}) async-start(f32[32,10,128]{2,1,0:T(8,128)} %broadcast_in_dim.47), calls=%async_computation.1 | async-start | bytes 524288 | tf_op jit(solution)/shard_map/all_to_all | solution.py:12
  40.4 0.1 eq.31
  40.5 10.5 %all-to-all-done.1 = f32[32,10,128]{2,1,0:T(8,128)} async-done(((f32[32,10,128]{2,1,0:T(8,128)}), f32[32,10,128]{2,1,0:T(8,128)}, u32[]{:S(2)}, u32[]{:S(2)}) %all-to-all-start.1) | async-done | bytes 163872 | tf_op jit(solution)/shard_map/all_to_all | solution.py:12
  51.0 0.9 slice_reduce_fusion.1
  51.9 0.5 slice.43
  52.4 1.7 %fusion.24 = (f32[]{:T(128)}, f32[128]{0:T(128)S(1)}) fusion(f32[2,128]{1,0:T(2,128)S(1)} %slice_reduce_fusion.1, f32[32,10,128]{2,1,0:T(8,128)} %all-to-all-done.1), kind=kOutput, calls=%fused_computation.59 | convolution fusion | flops 197119 | bytes 67076 | tf_op jit(solution)/shard_map/dot_general | solution.py:21
  54.1 0.3 fusion.21
  55.7 1.7 %fusion.4 = f32[]{:T(128)} fusion(f32[128]{0:T(128)S(1)} %get-tuple-element.10, f32[32,10,128]{2,1,0:T(8,128)} %all-to-all-done.1), kind=kOutput, calls=%fused_computation.9 | convolution fusion | flops 196863 | bytes 66564 | tf_op jit(solution)/shard_map/dot_general | solution.py:24
  58.1 0.5 fusion.12
  58.6 0.1 broadcast_multiply_fusion
  58.7 0.3 fusion.6
  59.0 12.7 %all_to_all.20 = f32[32,16,128]{2,1,0:T(8,128)S(1)} all-to-all(f32[32,16,128]{2,1,0:T(8,128)S(1)} %fusion.6), channel_id=1, replica_groups=mesh['blk'=8,'plane'=4] {'blk','plane'}, dimensions={0} | all-to-all | bytes 524288 | tf_op jit(solution)/shard_map/all_to_all | solution.py:12
  71.8 0.6 multiply_reduce_fusion.1
  72.4 1.8 %fusion.30 = f32[1,128]{1,0:T(1,128)S(1)} fusion(f32[2048,1]{0,1:T(1,128)S(1)} %bitcast.126, f32[2048,128]{1,0:T(8,128)} %param.15), kind=kOutput, calls=%fused_computation.65 | convolution fusion | flops 3145728 | bytes 1057280 | tf_op jit(solution)/shard_map/dot_general | solution.py:31
  74.2 0.7 stack.20
  74.9 0.6 broadcast_in_dim.49
  75.5 2.5 %all-to-all-start.3 = ((f32[32,2,128]{2,1,0:T(2,128)}), f32[32,2,128]{2,1,0:T(2,128)S(1)}, u32[]{:S(2)}, u32[]{:S(2)}) async-start(f32[32,2,128]{2,1,0:T(2,128)} %broadcast_in_dim.49), calls=%async_computation.3 | async-start | bytes 65536 | tf_op jit(solution)/shard_map/all_to_all | solution.py:12
  78.0 0.6 broadcast_multiply_fusion.1
  78.6 6.7 %all-to-all-done.3 = f32[32,2,128]{2,1,0:T(2,128)S(1)} async-done(((f32[32,2,128]{2,1,0:T(2,128)}), f32[32,2,128]{2,1,0:T(2,128)S(1)}, u32[]{:S(2)}, u32[]{:S(2)}) %all-to-all-start.3) | async-done | bytes 32800 | tf_op jit(solution)/shard_map/all_to_all | solution.py:12
  85.3 0.5 slice.47
  85.8 1.7 %fusion.19 = (f32[]{:T(128)}, f32[128]{0:T(128)S(1)}) fusion(f32[2,128]{1,0:T(2,128)S(1)} %reduce_sum.107, f32[32,10,128]{2,1,0:T(8,128)} %all-to-all-done.1), kind=kOutput, calls=%fused_computation.52 | convolution fusion | flops 197119 | bytes 67076 | tf_op jit(solution)/shard_map/dot_general | solution.py:21
  87.5 2.2 %fusion.16 = f32[1,2048]{1,0:T(1,128)S(1)} fusion(f32[2048,128]{1,0:T(8,128)} %param.15, f32[128]{0:T(128)S(1)} %get-tuple-element.12), kind=kOutput, calls=%fused_computation.47 | convolution fusion | flops 3145728 | bytes 1057280 | tf_op jit(solution)/shard_map/dot_general | solution.py:22
  91.0 1.7 %fusion.5 = f32[]{:T(128)} fusion(f32[128]{0:T(128)S(1)} %get-tuple-element.12, f32[32,10,128]{2,1,0:T(8,128)} %all-to-all-done.1), kind=kOutput, calls=%fused_computation.10 | convolution fusion | flops 196863 | bytes 66564 | tf_op jit(solution)/shard_map/dot_general | solution.py:24
  93.4 0.6 divide_multiply_fusion
  94.0 0.6 pad_maximum_fusion.1
  (15 shorter events, 0.2 us)
Async XLA Ops:
  0.6 30.6 %copy-start = (bf16[4,24,128,128]{3,2,1,0:T(8,128)(2,1)S(1)}, bf16[4,24,128,128]{3,2,1,0:T(8,128)(2,1)}, u32[]{:S(2)}) copy-start(bf16[4,24,128,128]{3,2,1,0:T(8,128)(2,1)} %param.8) | copy-start | bytes 9437188
  0.6 15.0 %copy-start.3 = (s32[4,24]{1,0:T(4,128)S(1)}, s32[4,24]{1,0:T(4,128)}, u32[]{:S(2)}) copy-start(s32[4,24]{1,0:T(4,128)} %param.9) | copy-start | bytes 1156
  0.7 15.1 %copy-start.4 = (s32[4]{0:T(128)S(1)}, s32[4]{0:T(128)}, u32[]{:S(2)}) copy-start(s32[4]{0:T(128)} %param.10) | copy-start | bytes 52
  5.0 29.4 %copy-start.1 = (f32[512,128]{1,0:T(8,128)S(1)}, f32[512,128]{1,0:T(8,128)}, u32[]{:S(2)}) copy-start(f32[512,128]{1,0:T(8,128)} %param.14) | copy-start | bytes 786436
  7.5 20.7 %all-to-all-start = ((f32[32,24,128]{2,1,0:T(8,128)}), f32[32,24,128]{2,1,0:T(8,128)}, u32[]{:S(2)}, u32[]{:S(2)}) async-start(f32[32,24,128]{2,1,0:T(8,128)} %pad_maximum_fusion), calls=%async_computation | async-start | bytes 786432 | tf_op jit(solution)/shard_map/all_to_all | solution.py:12
  33.0 38.8 %copy-start.2 = (f32[2048]{0:T(1024)S(1)}, f32[2048]{0:T(1024)}, u32[]{:S(2)}) copy-start(f32[2048]{0:T(1024)} %param.12) | copy-start | bytes 24580
  37.1 13.9 %all-to-all-start.1 = ((f32[32,10,128]{2,1,0:T(8,128)}), f32[32,10,128]{2,1,0:T(8,128)}, u32[]{:S(2)}, u32[]{:S(2)}) async-start(f32[32,10,128]{2,1,0:T(8,128)} %broadcast_in_dim.47), calls=%async_computation.1 | async-start | bytes 524288 | tf_op jit(solution)/shard_map/all_to_all | solution.py:12
  75.5 9.8 %all-to-all-start.3 = ((f32[32,2,128]{2,1,0:T(2,128)}), f32[32,2,128]{2,1,0:T(2,128)S(1)}, u32[]{:S(2)}, u32[]{:S(2)}) async-start(f32[32,2,128]{2,1,0:T(2,128)} %broadcast_in_dim.49), calls=%async_computation.3 | async-start | bytes 65536 | tf_op jit(solution)/shard_map/all_to_all | solution.py:12

commit v2 on v1

v2 whole, which is shorter than its diff:
```python
import math
from functools import partial

import jax
import jax.numpy as jnp
from jax import lax
from jax.experimental import pallas as pl
from jax.experimental.pallas import tpu as pltpu
from jax.sharding import PartitionSpec as P

AXES = ("blk", "plane")
F32 = jnp.float32


def exchange(parts):
    return lax.all_to_all(parts, AXES, 0, 0, tiled=True)


def column(row):
    size = row.shape[1]
    return jnp.broadcast_to(row, (size, size)).T


def left_times(row, mat):
    return jnp.sum(mat * column(row), axis=0, keepdims=True)


def right_times(mat, row):
    return jnp.sum((mat * row).T, axis=0, keepdims=True)


def total_of(row):
    return jnp.sum(row, axis=1, keepdims=True)


def forward_kernel(cols, counts, beta, got, tiles, basis, u_prev, payload, p_out, first, square):
    b = pl.program_id(0)
    share = payload.shape[1] - 2
    own = got.shape[1] - share
    slots, width = tiles.shape[1], tiles.shape[2]

    @pl.when(b == 0)
    def _():
        first[...] = jnp.zeros_like(first)
        square[...] = jnp.zeros_like(square)

    acc = jnp.zeros((width, width), F32)
    for s in range(slots):
        col = cols[b, s]
        row = got[lax.div(col, own), pl.ds(share + lax.rem(col, own), 1), :]
        row = jnp.where(s < counts[b], row, 0.0)
        acc = acc + tiles[0, s].astype(F32) * row
    p = jnp.sum(acc.T, axis=0, keepdims=True) - beta[0] * u_prev[pl.ds(b, 1), :]
    p_out[pl.ds(b, 1), :] = p
    first[...] += left_times(p, basis[0])
    square[...] += p * p

    @pl.when(b == pl.num_programs(0) - 1)
    def _():
        gram = jnp.sum(got[:, :share, :], axis=0)
        payload[:, :share, :] = jnp.broadcast_to(gram[None], (payload.shape[0],) + gram.shape)
        tail = (payload.shape[0], 1, width)
        payload[:, share : share + 1, :] = jnp.broadcast_to(first[...][None], tail)
        payload[:, share + 1 :, :] = jnp.broadcast_to(square[...][None], tail)


def solve(gram, sums):
    first = sums[0:1]
    coef = 2.0 * first - left_times(first, gram)
    total = (
        total_of(sums[1:2])
        - 2.0 * total_of(coef * first)
        + total_of(coef * left_times(coef, gram))
    )
    return coef, jnp.sqrt(total + 1e-06)


def fill_gram(gram, got, start, share):
    for d in range(gram.shape[0] // share):
        gram[d * share : (d + 1) * share, :] = got[start + d, :share, :]


def backward_kernel(
    cols, counts, got, p_in, tiles, basis, partial_out, u_out, alpha, gram, coef, *, scale
):
    b = pl.program_id(0)
    share = got.shape[1] - 2
    slots = tiles.shape[1]

    @pl.when(b == 0)
    def _():
        partial_out[...] = jnp.zeros_like(partial_out)
        fill_gram(gram, got, 0, share)
        found, norm = solve(gram[...], jnp.sum(got[:, share:, :], axis=0))
        coef[...] = found
        alpha[...] = jnp.broadcast_to(norm, alpha.shape)

    u = (p_in[pl.ds(b, 1), :] - right_times(basis[0], coef[...])) / alpha[...]
    u_out[pl.ds(b, 1), :] = u * scale
    spread = column(u.astype(jnp.bfloat16).astype(F32))
    for s in range(slots):
        part = jnp.sum(tiles[0, s].astype(F32) * spread, axis=0, keepdims=True)
        part = jnp.where(s < counts[b], part, 0.0)
        at = pl.ds(cols[b, s], 1)
        partial_out[at, :] = partial_out[at, :] + part


def inner_kernel(got, v_prev, alpha, basis, payload, r_out):
    r = jnp.sum(got[...], axis=0) - alpha[...] * v_prev[...]
    r_out[...] = r
    first = left_times(r[0:1], basis[0])
    for b in range(1, basis.shape[0]):
        first = first + left_times(r[b : b + 1], basis[b])
    tail = (payload.shape[0], 1, payload.shape[2])
    payload[:, 0:1, :] = jnp.broadcast_to(first[None], tail)
    square = jnp.sum(r * r, axis=0, keepdims=True)
    payload[:, 1:2, :] = jnp.broadcast_to(square[None], tail)


def final_kernel(got, grams, r_in, alpha, basis, v_out, coefs, gram, *, scale):
    share = grams.shape[1] - 2
    fill_gram(gram, grams, grams.shape[0] // 2, share)
    coef, norm = solve(gram[...], jnp.sum(got[...], axis=0))
    for b in range(basis.shape[0]):
        v = (r_in[b : b + 1, :] - right_times(basis[b], coef)) / norm
        v_out[b : b + 1, :] = v * scale
    coefs[0] = jnp.max(alpha[...])
    coefs[1] = jnp.max(norm)


def on_device(tiles, tile_cols, tile_count, u_start, v_start, beta_start, left_basis, right_basis):
    high = lax.Precision.HIGHEST
    devices = lax.axis_size(AXES)
    blocks, slots = tile_cols.shape
    width = tiles.shape[-1]
    kept = left_basis.shape[1]
    own = v_start.shape[0] // width
    n_tiles = own * devices
    left_scale = math.sqrt(u_start.shape[0] * devices)
    right_scale = math.sqrt(v_start.shape[0] * devices)
    share = 2 * kept // devices
    shape = jax.ShapeDtypeStruct
    smem = pl.BlockSpec(memory_space=pltpu.SMEM)
    vmem = pl.BlockSpec(memory_space=pltpu.VMEM)
    tile_spec = pl.BlockSpec((1, slots, width, width), lambda b: (b, 0, 0, 0))
    basis_spec = pl.BlockSpec((1, width, kept), lambda b: (b, 0, 0))
    left = left_basis.reshape(blocks, width, kept)
    right = right_basis.reshape(own, width, kept)
    row = pltpu.VMEM((1, kept), F32)

    grams = jnp.concatenate(
        [
            jnp.dot(left_basis.T, left_basis, precision=high),
            jnp.dot(right_basis.T, right_basis, precision=high),
        ]
    )
    v_rows = v_start.reshape(own, width)
    rounded = lax.reduce_precision(v_rows, 8, 7)
    got = exchange(
        jnp.concatenate(
            [
                grams.reshape(devices, share, kept),
                jnp.broadcast_to(rounded[None], (devices, own, width)),
            ],
            axis=1,
        )
    )
    payload, p = pl.pallas_call(
        forward_kernel,
        grid=(blocks,),
        in_specs=[smem, smem, smem, vmem, tile_spec, basis_spec, vmem],
        out_specs=[vmem, vmem],
        out_shape=[shape((devices, share + 2, width), F32), shape((blocks, width), F32)],
        scratch_shapes=[row, row],
        name="forward",
    )(tile_cols, tile_count, beta_start, got, tiles, left, u_start.reshape(blocks, width))
    sums = exchange(payload)
    partial_sums, u, alpha = pl.pallas_call(
        partial(backward_kernel, scale=left_scale),
        grid=(blocks,),
        in_specs=[smem, smem, vmem, vmem, tile_spec, basis_spec],
        out_specs=[vmem, vmem, vmem],
        out_shape=[
            shape((n_tiles, width), F32),
            shape((blocks, width), F32),
            shape((1, width), F32),
        ],
        scratch_shapes=[pltpu.VMEM((kept, kept), F32), row],
        name="backward",
    )(tile_cols, tile_count, sums, p, tiles, left)
    got = exchange(partial_sums.reshape(devices, own, width))
    payload, r = pl.pallas_call(
        inner_kernel,
        in_specs=[vmem] * 4,
        out_specs=[vmem, vmem],
        out_shape=[shape((devices, 2, width), F32), shape((own, width), F32)],
        name="inner",
    )(got, v_rows, alpha, right)
    v, coefs = pl.pallas_call(
        partial(final_kernel, scale=right_scale),
        in_specs=[vmem] * 5,
        out_specs=[vmem, smem],
        out_shape=[shape((own, width), F32), shape((2,), F32)],
        scratch_shapes=[pltpu.VMEM((kept, kept), F32)],
        name="final",
    )(exchange(payload), sums, r, alpha, right)
    return u.reshape(1, -1), v.reshape(1, -1), coefs


def solution(mesh):
    placed = (
        P(AXES, None, None, None),
        P(AXES, None),
        P(AXES),
        P(AXES),
        P(AXES),
        P(),
        P(AXES, None),
        P(AXES, None),
    )
    return jax.shard_map(
        on_device,
        mesh=mesh,
        in_specs=placed,
        out_specs=(P(None, AXES), P(None, AXES), P()),
        check_vma=False,
    )
```

time: 95.4 us -> 81.7 us (0.86)
  blocking collectives: 12.7 us -> 38.2 us
  waiting for transfers between devices: 29.5 us -> 12.6 us
  Pallas kernels: 0 us -> 14.3 us
  matrix products: 18.9 us -> 5.1 us
  other arithmetic: 8.45 us -> 1.5 us
  starting transfers between devices: 13.3 us -> 7.32 us
  local copies, waits for them, and re-layouts: 6.21 us -> 0.78 us
  between operations: 5.49 us -> 1.31 us
    all_to_all x1 -> x3, blocking collectives: 12.7 us -> 38.2 us  [exchange(): return lax.all_to_all(parts, AXES, 0, 0, tiled=True)]
    all_to_all x3 -> x1, waiting for transfers between devices: 29.5 us -> 12.6 us  [exchange(): return lax.all_to_all(parts, AXES, 0, 0, tiled=True)]
    pallas_call x0 -> x4, Pallas kernels: none -> 14.3 us  [the longest x1 4.9 us: on_device(): pl.pallas_call(partial(backward_kernel, scale=left_scale), grid=(blocks,)...]
    dot_general x11 -> x0, matrix products: 13.8 us -> none  [the longest x2 3.33 us: finish(): jnp.dot(gram, coef, precision=high)]
    all_to_all x3 -> x1, starting transfers between devices: 13.3 us -> 7.32 us  [exchange(): return lax.all_to_all(parts, AXES, 0, 0, tiled=True)]
    reduce_sum x7 -> x0, other arithmetic: 3.97 us -> none  [the longest x2 1.9 us: inner(): square = jnp.broadcast_to(jnp.sum(vec * vec), first.shape)]
    slice x3 -> x0, local copies, waits for them, and re-layouts: 2 us -> none  [the longest x2 1.03 us: on_device(): sums[1, 0]]
    broadcast_in_dim x4 -> x1, local copies, waits for them, and re-layouts: 1.43 us -> 0.02 us  [on_device(): jnp.broadcast_to(rounded[None], (devices, own, width))]
  transfers between devices with their start and end apart: 3 -> 1, of which waited for: 3 -> 1; matrix products, arithmetic and copies ran while one was open for 1% -> 0% of each run, Pallas kernels for 0% -> 0%
where the time goes in v2:
time: 81.7 us; the launch traced here: 81.1 us
  blocking collectives  38.2 us (47%)
  Pallas kernels  14.3 us (18%)
  waiting for transfers between devices  12.6 us (15%)
  starting transfers between devices  7.32 us (9%)
  matrix products  5.1 us (6%)
  other arithmetic  1.5 us (2%)
  between operations  1.31 us (2%)
    all_to_all x3, blocking collectives, exchange(): return lax.all_to_all(parts, AXES, 0, 0, tiled=True)  38.2 us
    all_to_all x1, waiting for transfers between devices, exchange(): return lax.all_to_all(parts, AXES, 0, 0, tiled=True)  12.6 us
    all_to_all x1, starting transfers between devices, exchange(): return lax.all_to_all(parts, AXES, 0, 0, tiled=True)  7.32 us
    pallas_call x1, Pallas kernels, on_device(): pl.pallas_call(partial(backward_kernel, scale=left_scale), grid=(blocks,)...  4.9 us
    pallas_call x1, Pallas kernels, on_device(): pl.pallas_call(forward_kernel, grid=(blocks,), in_specs=[smem, smem, smem...  4.44 us
    dot_general x1, matrix products, on_device(): jnp.dot(right_basis.T, right_basis, precision=high)  3.48 us
    pallas_call x1, Pallas kernels, on_device(): pl.pallas_call(partial(final_kernel, scale=right_scale), in_specs=[vmem]...  2.61 us
    pallas_call x1, Pallas kernels, on_device(): pl.pallas_call(inner_kernel, in_specs=[vmem] * 4, out_specs=[vmem, vmem],...  2.33 us
  transfers between devices with their start and end apart: 1, of which 1 were waited for; matrix products, arithmetic and copies ran while one was open for 0% of the time, Pallas kernels for 0%

profile of v2, /device:TPU:0, one launch (start us, length us, event | category | flops | bytes accessed | tf_op | source)
XLA Modules:
  0.0 81.1 jit_solution(3765180663386848427)
XLA Ops:
  0.6 0.7 bitcast_reduce-precision_fusion
  1.3 1.6 %fusion = f32[128,128]{1,0:T(8,128)S(1)} fusion(f32[512,128]{1,0:T(8,128)} %param.14), kind=kOutput, calls=%fused_computation.3 | convolution fusion | flops 100663296 | bytes 327680 | tf_op jit(solution)/shard_map/dot_general | solution.py:153
  3.0 3.5 %fusion.1 = f32[128,128]{1,0:T(8,128)S(1)} fusion(f32[2048,128]{1,0:T(8,128)} %param.15), kind=kOutput, calls=%fused_computation.4 | convolution fusion | flops 402653184 | bytes 1114112 | tf_op jit(solution)/shard_map/dot_general | solution.py:154
  6.5 0.8 pad_maximum_fusion
  7.3 7.3 %all-to-all-start = ((f32[32,24,128]{2,1,0:T(8,128)}), f32[32,24,128]{2,1,0:T(8,128)S(1)}, u32[]{:S(2)}, u32[]{:S(2)}) async-start(f32[32,24,128]{2,1,0:T(8,128)} %pad_maximum_fusion), calls=%async_computation | async-start | bytes 786432 | tf_op jit(solution)/shard_map/all_to_all | solution.py:16
  15.2 12.6 %all-to-all-done.got = f32[32,24,128]{2,1,0:T(8,128)S(1)} async-done(((f32[32,24,128]{2,1,0:T(8,128)}), f32[32,24,128]{2,1,0:T(8,128)S(1)}, u32[]{:S(2)}, u32[]{:S(2)}) %all-to-all-start) | async-done | bytes 393248 | tf_op jit(solution)/shard_map/all_to_all | solution.py:16
  27.8 0.0 copy-start
  27.8 0.8 copy-done
  28.6 4.4 %forward.1 = (f32[32,10,128]{2,1,0:T(8,128)}, f32[4,128]{1,0:T(4,128)}) custom-call(s32[4,24]{1,0:T(4,128)} %cols.3, s32[4]{0:T(128)} %counts.3, f32[1]{0:T(128)S(6)} %copy.11.beta, f32[32,24,128]{2,1,0:T(8,128)} %copy-done, bf16[4,24,128,128]{3,2,1,0:T(8,128)(2,1)} %tiles.3, f32[4,128,128]{2,1,0:T(8,128)} %bitcast.16, f32[4,128]{1,0:T(4,128)} %bitcast.20), custom_call_target="tpu_custom_call" | custom-call | tf_op jit(solution)/shard_map/forward/pallas_call | solution.py:168
  33.0 13.9 %all_to_all.20.got.grams = f32[32,10,128]{2,1,0:T(8,128)} all-to-all(f32[32,10,128]{2,1,0:T(8,128)} %get-tuple-element.12), channel_id=1, replica_groups=mesh['blk'=8,'plane'=4] {'blk','plane'}, dimensions={0} | all-to-all | bytes 327680 | tf_op jit(solution)/shard_map/all_to_all | solution.py:16
  46.9 4.9 %backward.1 = (f32[512,128]{1,0:T(8,128)}, f32[4,128]{1,0:T(4,128)}, f32[1,128]{1,0:T(1,128)}) custom-call(s32[4,24]{1,0:T(4,128)} %cols.3, s32[4]{0:T(128)} %counts.3, f32[32,10,128]{2,1,0:T(8,128)} %all_to_all.20.got.grams, f32[4,128]{1,0:T(4,128)} %get-tuple-element.13.p_in, bf16[4,24,128,128]{3,2,1,0:T(8,128)(2,1)} %tiles.3, f32[4,128,128]{2,1,0:T(8,128)} %bitcast.17), custom_call_target="tpu_custom_call" | custom-call | tf_op jit(solution)/shard_map/backward/pallas_call | solution.py:178
  51.8 13.9 %all_to_all.21.got = f32[32,16,128]{2,1,0:T(8,128)} all-to-all(f32[32,16,128]{2,1,0:T(8,128)} %bitcast.18), channel_id=1, replica_groups=mesh['blk'=8,'plane'=4] {'blk','plane'}, dimensions={0} | all-to-all | bytes 524288 | tf_op jit(solution)/shard_map/all_to_all | solution.py:16
  65.7 2.3 %inner.1 = (f32[32,2,128]{2,1,0:T(2,128)}, f32[16,128]{1,0:T(8,128)}) custom-call(f32[32,16,128]{2,1,0:T(8,128)} %all_to_all.21.got, f32[16,128]{1,0:T(8,128)} %bitcast.19, f32[1,128]{1,0:T(1,128)} %get-tuple-element.16.alpha, f32[16,128,128]{2,1,0:T(8,128)} %bitcast.14), custom_call_target="tpu_custom_call" | custom-call | tf_op jit(solution)/shard_map/inner/pallas_call | solution.py:192
  68.0 10.5 %all_to_all.22.got = f32[32,2,128]{2,1,0:T(2,128)} all-to-all(f32[32,2,128]{2,1,0:T(2,128)} %get-tuple-element.17), channel_id=1, replica_groups=mesh['blk'=8,'plane'=4] {'blk','plane'}, dimensions={0} | all-to-all | bytes 65536 | tf_op jit(solution)/shard_map/all_to_all | solution.py:16
  78.5 2.6 %final.1 = (f32[16,128]{1,0:T(8,128)}, f32[2]{0:T(128)}) custom-call(f32[32,2,128]{2,1,0:T(2,128)} %all_to_all.22.got, f32[32,10,128]{2,1,0:T(8,128)} %all_to_all.20.got.grams, f32[16,128]{1,0:T(8,128)} %get-tuple-element.18.r_in, f32[1,128]{1,0:T(1,128)} %get-tuple-element.16.alpha, f32[16,128,128]{2,1,0:T(8,128)} %bitcast.15), custom_call_target="tpu_custom_call" | custom-call | tf_op jit(solution)/shard_map/final/pallas_call | solution.py:199
  (2 shorter events, 0.0 us)
Async XLA Ops:
  7.3 20.6 %all-to-all-start = ((f32[32,24,128]{2,1,0:T(8,128)}), f32[32,24,128]{2,1,0:T(8,128)S(1)}, u32[]{:S(2)}, u32[]{:S(2)}) async-start(f32[32,24,128]{2,1,0:T(8,128)} %pad_maximum_fusion), calls=%async_computation | async-start | bytes 786432 | tf_op jit(solution)/shard_map/all_to_all | solution.py:16
  27.8 0.8 copy-start

commit v3 on v2

--- a/solution.py
+++ b/solution.py
@@ -33,10 +33,12 @@
     return jnp.sum(row, axis=1, keepdims=True)
 
 
-def forward_kernel(cols, counts, beta, got, tiles, basis, u_prev, payload, p_out, first, square):
+def forward_kernel(
+    cols, counts, beta, got, tiles, basis, u_prev, payload, p_out, kept_rows, first, square
+):
     b = pl.program_id(0)
     share = payload.shape[1] - 2
-    own = got.shape[1] - share
+    own = got.shape[1] - 2 * share
     slots, width = tiles.shape[1], tiles.shape[2]
 
     @pl.when(b == 0)
@@ -47,7 +49,7 @@
     acc = jnp.zeros((width, width), F32)
     for s in range(slots):
         col = cols[b, s]
-        row = got[lax.div(col, own), pl.ds(share + lax.rem(col, own), 1), :]
+        row = got[lax.div(col, own), pl.ds(2 * share + lax.rem(col, own), 1), :]
         row = jnp.where(s < counts[b], row, 0.0)
         acc = acc + tiles[0, s].astype(F32) * row
     p = jnp.sum(acc.T, axis=0, keepdims=True) - beta[0] * u_prev[pl.ds(b, 1), :]
@@ -59,6 +61,7 @@
     def _():
         gram = jnp.sum(got[:, :share, :], axis=0)
         payload[:, :share, :] = jnp.broadcast_to(gram[None], (payload.shape[0],) + gram.shape)
+        kept_rows[...] = jnp.sum(got[:, share : 2 * share, :], axis=0)
         tail = (payload.shape[0], 1, width)
         payload[:, share : share + 1, :] = jnp.broadcast_to(first[...][None], tail)
         payload[:, share + 1 :, :] = jnp.broadcast_to(square[...][None], tail)
@@ -75,9 +78,9 @@
     return coef, jnp.sqrt(total + 1e-06)
 
 
-def fill_gram(gram, got, start, share):
+def fill_gram(gram, got, share):
     for d in range(gram.shape[0] // share):
-        gram[d * share : (d + 1) * share, :] = got[start + d, :share, :]
+        gram[d * share : (d + 1) * share, :] = got[d, :share, :]
 
 
 def backward_kernel(
@@ -90,7 +93,7 @@
     @pl.when(b == 0)
     def _():
         partial_out[...] = jnp.zeros_like(partial_out)
-        fill_gram(gram, got, 0, share)
+        fill_gram(gram, got, share)
         found, norm = solve(gram[...], jnp.sum(got[:, share:, :], axis=0))
         coef[...] = found
         alpha[...] = jnp.broadcast_to(norm, alpha.shape)
@@ -105,22 +108,26 @@
         partial_out[at, :] = partial_out[at, :] + part
 
 
-def inner_kernel(got, v_prev, alpha, basis, payload, r_out):
+def inner_kernel(got, v_prev, alpha, basis, gram_rows, payload, r_out):
+    share = gram_rows.shape[0]
     r = jnp.sum(got[...], axis=0) - alpha[...] * v_prev[...]
     r_out[...] = r
     first = left_times(r[0:1], basis[0])
     for b in range(1, basis.shape[0]):
         first = first + left_times(r[b : b + 1], basis[b])
     tail = (payload.shape[0], 1, payload.shape[2])
-    payload[:, 0:1, :] = jnp.broadcast_to(first[None], tail)
+    payload[:, :share, :] = jnp.broadcast_to(
+        gram_rows[...][None], (payload.shape[0],) + gram_rows.shape
+    )
+    payload[:, share : share + 1, :] = jnp.broadcast_to(first[None], tail)
     square = jnp.sum(r * r, axis=0, keepdims=True)
-    payload[:, 1:2, :] = jnp.broadcast_to(square[None], tail)
-
-
-def final_kernel(got, grams, r_in, alpha, basis, v_out, coefs, gram, *, scale):
-    share = grams.shape[1] - 2
-    fill_gram(gram, grams, grams.shape[0] // 2, share)
-    coef, norm = solve(gram[...], jnp.sum(got[...], axis=0))
+    payload[:, share + 1 :, :] = jnp.broadcast_to(square[None], tail)
+
+
+def final_kernel(got, r_in, alpha, basis, v_out, coefs, gram, *, scale):
+    share = got.shape[1] - 2
+    fill_gram(gram, got, share)
+    coef, norm = solve(gram[...], jnp.sum(got[:, share:, :], axis=0))
     for b in range(basis.shape[0]):
         v = (r_in[b : b + 1, :] - right_times(basis[b], coef)) / norm
         v_out[b : b + 1, :] = v * scale
@@ -138,7 +145,7 @@
     n_tiles = own * devices
     left_scale = math.sqrt(u_start.shape[0] * devices)
     right_scale = math.sqrt(v_start.shape[0] * devices)
-    share = 2 * kept // devices
+    share = pl.cdiv(kept, devices)
     shape = jax.ShapeDtypeStruct
     smem = pl.BlockSpec(memory_space=pltpu.SMEM)
     vmem = pl.BlockSpec(memory_space=pltpu.VMEM)
@@ -148,29 +155,33 @@
     right = right_basis.reshape(own, width, kept)
     row = pltpu.VMEM((1, kept), F32)
 
-    grams = jnp.concatenate(
-        [
-            jnp.dot(left_basis.T, left_basis, precision=high),
-            jnp.dot(right_basis.T, right_basis, precision=high),
-        ]
-    )
+    def shares(basis):
+        gram = jnp.dot(basis.T, basis, precision=high)
+        gram = jnp.pad(gram, ((0, share * devices - kept), (0, 0)))
+        return gram.reshape(devices, share, kept)
+
     v_rows = v_start.reshape(own, width)
     rounded = lax.reduce_precision(v_rows, 8, 7)
     got = exchange(
         jnp.concatenate(
             [
-                grams.reshape(devices, share, kept),
+                shares(left_basis),
+                shares(right_basis),
                 jnp.broadcast_to(rounded[None], (devices, own, width)),
             ],
             axis=1,
         )
     )
-    payload, p = pl.pallas_call(
+    payload, p, kept_rows = pl.pallas_call(
         forward_kernel,
         grid=(blocks,),
         in_specs=[smem, smem, smem, vmem, tile_spec, basis_spec, vmem],
-        out_specs=[vmem, vmem],
-        out_shape=[shape((devices, share + 2, width), F32), shape((blocks, width), F32)],
+        out_specs=[vmem, vmem, vmem],
+        out_shape=[
+            shape((devices, share + 2, width), F32),
+            shape((blocks, width), F32),
+            shape((share, width), F32),
+        ],
         scratch_shapes=[row, row],
         name="forward",
     )(tile_cols, tile_count, beta_start, got, tiles, left, u_start.reshape(blocks, width))
@@ -191,19 +202,19 @@
     got = exchange(partial_sums.reshape(devices, own, width))
     payload, r = pl.pallas_call(
         inner_kernel,
-        in_specs=[vmem] * 4,
+        in_specs=[vmem] * 5,
         out_specs=[vmem, vmem],
-        out_shape=[shape((devices, 2, width), F32), shape((own, width), F32)],
+        out_shape=[shape((devices, share + 2, width), F32), shape((own, width), F32)],
         name="inner",
-    )(got, v_rows, alpha, right)
+    )(got, v_rows, alpha, right, kept_rows)
     v, coefs = pl.pallas_call(
         partial(final_kernel, scale=right_scale),
-        in_specs=[vmem] * 5,
+        in_specs=[vmem] * 4,
         out_specs=[vmem, smem],
         out_shape=[shape((own, width), F32), shape((2,), F32)],
         scratch_shapes=[pltpu.VMEM((kept, kept), F32)],
         name="final",
-    )(exchange(payload), sums, r, alpha, right)
+    )(exchange(payload), r, alpha, right)
     return u.reshape(1, -1), v.reshape(1, -1), coefs
 
 

time: 81.7 us -> 80.2 us (0.982)
  blocking collectives: 38.2 us -> 36.8 us
    all_to_all x3, blocking collectives: 38.2 us -> 36.8 us  [exchange(): return lax.all_to_all(parts, AXES, 0, 0, tiled=True)]
where the time goes in v3:
time: 80.2 us; the launch traced here: 79.6 us
  blocking collectives  36.8 us (46%)
  Pallas kernels  14.2 us (18%)
  waiting for transfers between devices  12.6 us (16%)
  starting transfers between devices  7.32 us (9%)
  matrix products  5.1 us (6%)
  other arithmetic  1.51 us (2%)
  between operations  1.31 us (2%)
    all_to_all x3, blocking collectives, exchange(): return lax.all_to_all(parts, AXES, 0, 0, tiled=True)  36.8 us
    all_to_all x1, waiting for transfers between devices, exchange(): return lax.all_to_all(parts, AXES, 0, 0, tiled=True)  12.6 us
    all_to_all x1, starting transfers between devices, exchange(): return lax.all_to_all(parts, AXES, 0, 0, tiled=True)  7.32 us
    dot_general x2, matrix products, shares(): gram = jnp.dot(basis.T, basis, precision=high)  5.1 us
    pallas_call x1, Pallas kernels, on_device(): pl.pallas_call(partial(backward_kernel, scale=left_scale), grid=(blocks,)...  4.86 us
    pallas_call x1, Pallas kernels, on_device(): pl.pallas_call(forward_kernel, grid=(blocks,), in_specs=[smem, smem, smem...  4.4 us
    pallas_call x1, Pallas kernels, on_device(): pl.pallas_call(partial(final_kernel, scale=right_scale), in_specs=[vmem]...  2.59 us
    pallas_call x1, Pallas kernels, on_device(): pl.pallas_call(inner_kernel, in_specs=[vmem] * 5, out_specs=[vmem, vmem],...  2.33 us
  transfers between devices with their start and end apart: 1, of which 1 were waited for; matrix products, arithmetic and copies ran while one was open for 0% of the time, Pallas kernels for 0%

profile of v3, /device:TPU:0, one launch (start us, length us, event | category | flops | bytes accessed | tf_op | source)
XLA Modules:
  0.0 79.6 jit_solution(12800795154980103358)
XLA Ops:
  0.6 0.7 bitcast_reduce-precision_fusion
  1.3 1.6 %fusion = f32[128,128]{1,0:T(8,128)S(1)} fusion(f32[512,128]{1,0:T(8,128)} %param.14), kind=kOutput, calls=%fused_computation.2 | convolution fusion | flops 100663296 | bytes 327680 | tf_op jit(solution)/shard_map/dot_general | solution.py:159
  3.0 3.5 %fusion.1 = f32[128,128]{1,0:T(8,128)S(1)} fusion(f32[2048,128]{1,0:T(8,128)} %param.15), kind=kOutput, calls=%fused_computation.3 | convolution fusion | flops 402653184 | bytes 1114112 | tf_op jit(solution)/shard_map/dot_general | solution.py:159
  6.5 0.8 %pad_maximum_fusion = f32[32,24,128]{2,1,0:T(8,128)} fusion(f32[32,16,128]{2,1,0:T(8,128)S(1)} %broadcast_in_dim.2, f32[32,4,128]{2,1,0:T(4,128)S(1)} %bitcast.19, f32[32,4,128]{2,1,0:T(4,128)S(1)} %bitcast.18), kind=kLoop, calls=%fused_computation | loop fusion | flops 196608 | bytes 786432 | tf_op jit(solution)/shard_map/concatenate | solution.py:166
  7.3 7.3 %all-to-all-start = ((f32[32,24,128]{2,1,0:T(8,128)}), f32[32,24,128]{2,1,0:T(8,128)S(1)}, u32[]{:S(2)}, u32[]{:S(2)}) async-start(f32[32,24,128]{2,1,0:T(8,128)} %pad_maximum_fusion), calls=%async_computation | async-start | bytes 786432 | tf_op jit(solution)/shard_map/all_to_all | solution.py:16
  15.3 12.6 %all-to-all-done.got = f32[32,24,128]{2,1,0:T(8,128)S(1)} async-done(((f32[32,24,128]{2,1,0:T(8,128)}), f32[32,24,128]{2,1,0:T(8,128)S(1)}, u32[]{:S(2)}, u32[]{:S(2)}) %all-to-all-start) | async-done | bytes 393248 | tf_op jit(solution)/shard_map/all_to_all | solution.py:16
  27.8 0.0 copy-start
  27.9 0.8 copy-done
  28.6 4.4 %forward.1 = (f32[32,6,128]{2,1,0:T(8,128)}, f32[4,128]{1,0:T(4,128)}, f32[4,128]{1,0:T(4,128)}) custom-call(s32[4,24]{1,0:T(4,128)} %cols.3, s32[4]{0:T(128)} %counts.3, f32[1]{0:T(128)S(6)} %copy.11.beta, f32[32,24,128]{2,1,0:T(8,128)} %copy-done, bf16[4,24,128,128]{3,2,1,0:T(8,128)(2,1)} %tiles.3, f32[4,128,128]{2,1,0:T(8,128)} %bitcast.16, f32[4,128]{1,0:T(4,128)} %bitcast.22), custom_call_target="tpu_custom_call" | custom-call | tf_op jit(solution)/shard_map/forward/pallas_call | solution.py:175
  33.0 11.5 %all_to_all.20.got = f32[32,6,128]{2,1,0:T(8,128)} all-to-all(f32[32,6,128]{2,1,0:T(8,128)} %get-tuple-element.13), channel_id=1, replica_groups=mesh['blk'=8,'plane'=4] {'blk','plane'}, dimensions={0} | all-to-all | bytes 196608 | tf_op jit(solution)/shard_map/all_to_all | solution.py:16
  44.5 4.9 %backward.1 = (f32[512,128]{1,0:T(8,128)}, f32[4,128]{1,0:T(4,128)}, f32[1,128]{1,0:T(1,128)}) custom-call(s32[4,24]{1,0:T(4,128)} %cols.3, s32[4]{0:T(128)} %counts.3, f32[32,6,128]{2,1,0:T(8,128)} %all_to_all.20.got, f32[4,128]{1,0:T(4,128)} %get-tuple-element.14.p_in, bf16[4,24,128,128]{3,2,1,0:T(8,128)(2,1)} %tiles.3, f32[4,128,128]{2,1,0:T(8,128)} %bitcast.17), custom_call_target="tpu_custom_call" | custom-call | tf_op jit(solution)/shard_map/backward/pallas_call | solution.py:189
  49.3 13.9 %all_to_all.21.got = f32[32,16,128]{2,1,0:T(8,128)} all-to-all(f32[32,16,128]{2,1,0:T(8,128)} %bitcast.20), channel_id=1, replica_groups=mesh['blk'=8,'plane'=4] {'blk','plane'}, dimensions={0} | all-to-all | bytes 524288 | tf_op jit(solution)/shard_map/all_to_all | solution.py:16
  63.2 2.3 %inner.1 = (f32[32,6,128]{2,1,0:T(8,128)}, f32[16,128]{1,0:T(8,128)}) custom-call(f32[32,16,128]{2,1,0:T(8,128)} %all_to_all.21.got, f32[16,128]{1,0:T(8,128)} %bitcast.21, f32[1,128]{1,0:T(1,128)} %get-tuple-element.17.alpha, f32[16,128,128]{2,1,0:T(8,128)} %bitcast.14, f32[4,128]{1,0:T(4,128)} %get-tuple-element.18.gram_rows), custom_call_target="tpu_custom_call" | custom-call | tf_op jit(solution)/shard_map/inner/pallas_call | solution.py:203
  65.5 11.5 %all_to_all.22.got = f32[32,6,128]{2,1,0:T(8,128)} all-to-all(f32[32,6,128]{2,1,0:T(8,128)} %get-tuple-element.19), channel_id=1, replica_groups=mesh['blk'=8,'plane'=4] {'blk','plane'}, dimensions={0} | all-to-all | bytes 196608 | tf_op jit(solution)/shard_map/all_to_all | solution.py:16
  77.0 2.6 %final.1 = (f32[16,128]{1,0:T(8,128)}, f32[2]{0:T(128)}) custom-call(f32[32,6,128]{2,1,0:T(8,128)} %all_to_all.22.got, f32[16,128]{1,0:T(8,128)} %get-tuple-element.20.r_in, f32[1,128]{1,0:T(1,128)} %get-tuple-element.17.alpha, f32[16,128,128]{2,1,0:T(8,128)} %bitcast.15), custom_call_target="tpu_custom_call" | custom-call | tf_op jit(solution)/shard_map/final/pallas_call | solution.py:210
  (1 shorter events, 0.0 us)
Async XLA Ops:
  7.3 20.6 %all-to-all-start = ((f32[32,24,128]{2,1,0:T(8,128)}), f32[32,24,128]{2,1,0:T(8,128)S(1)}, u32[]{:S(2)}, u32[]{:S(2)}) async-start(f32[32,24,128]{2,1,0:T(8,128)} %pad_maximum_fusion), calls=%async_computation | async-start | bytes 786432 | tf_op jit(solution)/shard_map/all_to_all | solution.py:16
  27.8 0.8 copy-start
